TPU v7x, 32 devices: a whole 2x2x4 slice. The times are simulated.
32 devices in a mesh: query: 8 (over z, y), tensor: 2 (over x), dp: 2 (over core).
Axes of the slice: x: 2, y: 2, z: 4, core: 2. Of those that a mesh axis runs over, the one named last changes fastest.
Arguments:
- hidden: bfloat16 [16, 1024, 14336], P(('query', 'dp'), None, 'tensor'), may hold values from -6 to 6
- out_grad: bfloat16 [16, 1024, 4096], P(('query', 'dp'), None, 'tensor'), may hold values from -6 to 6
- proj_in: bfloat16 [14336, 64], P('tensor'), may hold values from -0.046875 to 0.046875
- proj_out: bfloat16 [4096, 64], P('tensor'), may hold values from -0.09375 to 0.09375
- seg_ids: int32 [16, 1024], P(('query', 'dp')), may hold values from 0 to 31, never falling along the last dimension, each value on 1 to 288 neighbouring positions
- queries: bfloat16 [1024, 4096], P(('query', 'dp'), 'tensor'), may hold values from -0.01171875 to 0.01171875
Outputs:
- scores: float32 [512, 1024], P('tensor', ('query', 'dp'))
All inputs are finite; a program needn't handle non-finite values.
Results may differ from a plain program's by a relative error of at most 0.004.
Values may be sent and summed in bfloat16 or wider, within the bound.
No kernel may reach another device: no remote copies, remote signals or barrier semaphores. Data moves between devices by JAX's collectives and lax.ppermute only.
A program may use at most 64 MiB of HBM per device.

v0:
```python
import jax
import jax.numpy as jnp
from jax import lax
from jax.sharding import PartitionSpec as P

SEGS = 32


def local(hidden, out_grad, proj_in, proj_out, seg_ids, queries):
    tokens = hidden[0]
    grads = out_grad[0]
    segment = seg_ids[0]
    part_in = jnp.dot(tokens, proj_in, preferred_element_type=jnp.float32)
    part_out = jnp.dot(grads, proj_out, preferred_element_type=jnp.float32)
    act_proj = lax.psum(part_in, "tensor")
    grad_share = lax.psum_scatter(part_out, "tensor", scatter_dimension=1, tiled=True)
    outer = (
        (grad_share[:, :, None] * act_proj[:, None, :])
        .reshape(tokens.shape[0], -1)
        .astype(jnp.bfloat16)
    )
    member = (segment[None, :] == jnp.arange(SEGS, dtype=jnp.int32)[:, None]).astype(jnp.bfloat16)
    doc_feats = jnp.dot(member, outer, preferred_element_type=jnp.float32).astype(jnp.bfloat16)
    table = lax.dot_general(
        lax.all_gather(doc_feats, ("query", "dp"), axis=0, tiled=True),
        queries,
        (((1,), (1,)), ((), ())),
        preferred_element_type=jnp.float32,
    )
    return lax.psum_scatter(table, "tensor", scatter_dimension=0, tiled=True)


def solution(mesh):
    in_specs = (
        P(("query", "dp"), None, "tensor"),
        P(("query", "dp"), None, "tensor"),
        P("tensor", None),
        P("tensor", None),
        P(("query", "dp"), None),
        P(("query", "dp"), "tensor"),
    )
    out_specs = P("tensor", ("query", "dp"))
    return jax.shard_map(local, mesh=mesh, in_specs=in_specs, out_specs=out_specs, check_vma=False)
```

profile of v0, /device:TPU:0, one launch (start us, length us, event | category | flops | bytes accessed | tf_op | source)
XLA Modules:
  0.0 123.0 jit_solution(5992180469758918118)
XLA Ops:
  6.5 0.0 copy-start
  6.5 0.0 copy-start.1
  6.5 0.0 all-reduce.2.cloned.1.call-start
  6.5 1.2 copy-done
  7.7 10.4 %fusion = f32[1024,64]{0,1:T(8,128)} fusion(bf16[7168,64]{0,1:T(8,128)(2,1)S(1)} %copy-done, bf16[1,1024,7168]{2,1,0:T(8,128)(2,1)} %param.6), kind=kOutput, calls=%fused_computation | convolution fusion | flops 939524096 | bytes 15859712 | tf_op jit(solution)/shard_map/dot_general | solution.py:13
  18.1 0.0 all-reduce.2.cloned.1.call-update
  18.2 0.0 copy-start.3
  18.2 0.0 reduce-scatter.3.cloned.1.call-start
  18.2 0.0 copy-done.1
  18.2 4.3 %fusion.2 = f32[1024,64]{0,1:T(8,128)} fusion(bf16[2048,64]{0,1:T(8,128)(2,1)S(1)} %copy-done.1, bf16[1,1024,2048]{2,1,0:T(8,128)(2,1)} %param.7), kind=kOutput, calls=%fused_computation.3 | convolution fusion | flops 268435456 | bytes 4718592 | tf_op jit(solution)/shard_map/dot_general | solution.py:14
  22.5 0.0 reduce-scatter.3.cloned.1.call-update
  22.5 0.0 copy-start.2
  22.6 0.0 all-gather.2.cloned.1.call-start
  22.6 21.7 %all-reduce.2.cloned.1.call-done = f32[1024,64]{0,1:T(8,128)} async-done(((f32[1024,64]{0,1:T(8,128)}), f32[1024,64]{0,1:T(8,128)}) %all-reduce.2.cloned.1.call-update) | async-done | bytes 262160 | tf_op jit(solution)/shard_map/psum | solution.py:15
  44.3 14.0 %reduce-scatter.3.cloned.1.call-done = f32[1024,32]{0,1:T(8,128)} async-done(((f32[1024,64]{0,1:T(8,128)}), f32[1024,32]{0,1:T(8,128)}) %reduce-scatter.3.cloned.1.call-update) | async-done | bytes 131088 | tf_op jit(solution)/shard_map/reduce_scatter | solution.py:16
  58.4 2.2 %multiply_convert_fusion = bf16[1024,32,64]{0,2,1:T(8,128)(2,1)S(1)} fusion(f32[1024,64]{0,1:T(8,128)} %all-reduce.2.cloned.1.call-done, f32[1024,32]{0,1:T(8,128)} %reduce-scatter.3.cloned.1.call-done), kind=kLoop, calls=%fused_computation.2 | loop fusion | flops 4194304 | bytes 4587520 | tf_op jit(solution)/shard_map/convert_element_type | solution.py:20
  60.6 0.0 copy-done.3
  60.6 2.0 %convolution_convert_fusion = bf16[32,2048]{1,0:T(8,128)(2,1)} fusion(bf16[1024,2048]{0,1:T(8,128)(2,1)S(1)} %bitcast.13, s32[1024]{0:T(1024)S(1)} %bitcast.14), kind=kOutput, calls=%fused_computation.5 | convolution fusion | flops 134316032 | bytes 4329472 | tf_op jit(solution)/shard_map/dot_general | solution.py:23
  62.6 0.0 all-gather.2.cloned.1.call-update
  62.6 0.0 reduce-scatter.5.cloned.1.call-start
  62.7 41.6 %all-gather.2.cloned.1.call-done = bf16[512,2048]{1,0:T(8,128)(2,1)} async-done(((bf16[32,2048]{1,0:T(8,128)(2,1)}), bf16[512,2048]{1,0:T(8,128)(2,1)}) %all-gather.2.cloned.1.call-update) | async-done | bytes 2097168 | tf_op jit(solution)/shard_map/all_gather | solution.py:25
  104.2 0.0 copy-done.2
  104.2 3.0 %fusion.5 = f32[512,64]{0,1:T(8,128)} fusion(bf16[512,2048]{1,0:T(8,128)(2,1)} %all-gather.2.cloned.1.call-done, bf16[64,2048]{1,0:T(8,128)(2,1)S(1)} %copy-done.2), kind=kOutput, calls=%fused_computation.8 | convolution fusion | flops 134217728 | bytes 2490368 | tf_op jit(solution)/shard_map/dot_general | solution.py:24
  107.2 0.0 reduce-scatter.5.cloned.1.call-update
  107.3 9.2 %reduce-scatter.5.cloned.1.call-done = f32[256,64]{0,1:T(8,128)} async-done(((f32[512,64]{0,1:T(8,128)}), f32[256,64]{0,1:T(8,128)}) %reduce-scatter.5.cloned.1.call-update) | async-done | bytes 65552 | tf_op jit(solution)/shard_map/reduce_scatter | solution.py:30
Async XLA Ops:
  6.5 1.2 copy-start
  6.5 11.7 %copy-start.1 = (bf16[2048,64]{0,1:T(8,128)(2,1)S(1)}, bf16[2048,64]{0,1:T(8,128)(2,1)}, u32[]{:S(2)}) copy-start(bf16[2048,64]{0,1:T(8,128)(2,1)} %param.9) | copy-start | bytes 786436
  6.5 37.8 %all-reduce.2.cloned.1.call-start = ((), (), s32[]{:S(2)}) async-start(), calls=%async_computation.3 | async-start | bytes 524288 | tf_op jit(solution)/shard_map/psum | solution.py:15
  18.2 42.5 %copy-start.3 = (s32[1,1024]{1,0:T(1,128)S(1)}, s32[1,1024]{1,0:T(1,128)}, u32[]{:S(2)}) copy-start(s32[1,1024]{1,0:T(1,128)} %param.10) | copy-start | bytes 12292
  18.2 40.2 %reduce-scatter.3.cloned.1.call-start = ((), (), s32[]{:S(2)}) async-start(), calls=%async_computation.2 | async-start | bytes 393216 | tf_op jit(solution)/shard_map/reduce_scatter | solution.py:16
  22.5 81.7 %copy-start.2 = (bf16[64,2048]{1,0:T(8,128)(2,1)S(1)}, bf16[64,2048]{1,0:T(8,128)(2,1)}, u32[]{:S(2)}) copy-start(bf16[64,2048]{1,0:T(8,128)(2,1)} %param.11) | copy-start | bytes 786436
  22.6 81.7 %all-gather.2.cloned.1.call-start = ((), (), s32[]{:S(2)}) async-start(), calls=%async_computation.4 | async-start | bytes 2228224 | tf_op jit(solution)/shard_map/all_gather | solution.py:25
  62.6 53.9 %reduce-scatter.5.cloned.1.call-start = ((), (), s32[]{:S(2)}) async-start(), calls=%async_computation.5 | async-start | bytes 196608 | tf_op jit(solution)/shard_map/reduce_scatter | solution.py:30
Sparse Core Ops, SparseCore 0:
  18.3 26.0 all-reduce.1
  46.6 11.7 reduce-scatter.2
  62.7 41.4 all-gather.1
  107.4 9.0 reduce-scatter.4
where the time goes:
time: 123 us
  waiting for transfers between devices  86.6 us (70%)
  matrix products  19.7 us (16%)
  between operations  13.2 us (11%)
  other arithmetic  2.24 us (2%)
    all_gather x1, waiting for transfers between devices, local(): lax.all_gather(doc_feats, ('query', 'dp'), axis=0, tiled=True)  41.6 us
    psum x1, waiting for transfers between devices, local(): act_proj = lax.psum(part_in, 'tensor')  21.7 us
    reduce_scatter x1, waiting for transfers between devices, local(): lax.psum_scatter(part_out, 'tensor', scatter_dimension=1, tiled=True)  14 us
    dot_general x1, matrix products, local(): part_in = jnp.dot(tokens, proj_in, preferred_element_type=jnp.float32)  10.4 us
    reduce_scatter x1, waiting for transfers between devices, local(): return lax.psum_scatter(table, 'tensor', scatter_dimension=0, tiled=True)  9.23 us
    dot_general x1, matrix products, local(): part_out = jnp.dot(grads, proj_out, preferred_element_type=jnp.float32)  4.28 us
    dot_general x1, matrix products, local(): lax.dot_general(lax.all_gather(doc_feats, ('query', 'dp'), axis=0, tiled=...  3 us
  transfers between devices with their start and end apart: 4, of which 4 were waited for; matrix products, arithmetic and copies ran while one was open for 3% of the time, Pallas kernels for 0%

commit v1 on v0

--- a/solution.py
+++ b/solution.py
@@ -12,7 +12,8 @@
     segment = seg_ids[0]
     part_in = jnp.dot(tokens, proj_in, preferred_element_type=jnp.float32)
     part_out = jnp.dot(grads, proj_out, preferred_element_type=jnp.float32)
-    act_proj = lax.psum(part_in, "tensor")
+    terms = lax.all_gather(part_in, "tensor")
+    act_proj = jnp.sum(terms, axis=0)
     grad_share = lax.psum_scatter(part_out, "tensor", scatter_dimension=1, tiled=True)
     outer = (
         (grad_share[:, :, None] * act_proj[:, None, :])

time: 123 us -> 98.2 us (0.80)
  waiting for transfers between devices: 86.6 us -> 52.4 us
  blocking collectives: 0 us -> 10.1 us
    psum x1 -> x0, waiting for transfers between devices: 21.7 us -> none  [local(): act_proj = lax.psum(part_in, 'tensor')]
    reduce_scatter x1, waiting for transfers between devices: 14 us -> 0.02 us  [local(): lax.psum_scatter(part_out, 'tensor', scatter_dimension=1, tiled=True)]
    all_gather x0 -> x1, blocking collectives: none -> 10.1 us  [local(): terms = lax.all_gather(part_in, 'tensor')]
    all_gather x1, waiting for transfers between devices: 41.6 us -> 43.1 us  [local(): lax.all_gather(doc_feats, ('query', 'dp'), axis=0, tiled=True)]
  transfers between devices with their start and end apart: 4 -> 3, of which waited for: 4 -> 2; matrix products, arithmetic and copies ran while one was open for 3% -> 11% of each run, Pallas kernels for 0% -> 0%
where the time goes in v1:
time: 98.2 us; the launch traced here: 98 us
  waiting for transfers between devices  52.4 us (53%)
  matrix products  19.1 us (19%)
  between operations  13.2 us (13%)
  blocking collectives  10.1 us (10%)
  other arithmetic  2.81 us (3%)
    all_gather x1, waiting for transfers between devices, local(): lax.all_gather(doc_feats, ('query', 'dp'), axis=0, tiled=True)  43.1 us
    all_gather x1, blocking collectives, local(): terms = lax.all_gather(part_in, 'tensor')  10.1 us
    dot_general x1, matrix products, local(): part_in = jnp.dot(tokens, proj_in, preferred_element_type=jnp.float32)  9.73 us
    reduce_scatter x1, waiting for transfers between devices, local(): return lax.psum_scatter(table, 'tensor', scatter_dimension=0, tiled=True)  9.23 us
    dot_general x1, matrix products, local(): part_out = jnp.dot(grads, proj_out, preferred_element_type=jnp.float32)  4.38 us
    dot_general x1, matrix products, local(): lax.dot_general(lax.all_gather(doc_feats, ('query', 'dp'), axis=0, tiled=...  3 us
    convert_element_type x1, other arithmetic, local(): outer = (grad_share[:, :, None] * act_proj[:, None, :]).reshape(tokens.sh...  2.19 us
    dot_general x1, matrix products, local(): jnp.dot(member, outer, preferred_element_type=jnp.float32)  1.97 us
  transfers between devices with their start and end apart: 3, of which 2 were waited for; matrix products, arithmetic and copies ran while one was open for 11% of the time, Pallas kernels for 0%

profile of v1, /device:TPU:0, one launch (start us, length us, event | category | flops | bytes accessed | tf_op | source)
XLA Modules:
  0.0 98.0 jit_solution(13894252885614121842)
XLA Ops:
  6.5 0.0 copy-start
  6.5 0.0 reduce-scatter.3.cloned.1.call-start
  6.5 4.4 %fusion.2 = f32[1024,64]{0,1:T(8,128)} fusion(bf16[2048,64]{0,1:T(8,128)(2,1)} %param.9, bf16[1,1024,2048]{2,1,0:T(8,128)(2,1)} %param.7), kind=kOutput, calls=%fused_computation.3 | convolution fusion | flops 268435456 | bytes 4718592 | tf_op jit(solution)/shard_map/dot_general | solution.py:14
  10.9 0.0 reduce-scatter.3.cloned.1.call-update
  10.9 0.0 all-gather.3.cloned.1.call-start
  11.0 0.0 copy-done
  11.0 9.7 %fusion = f32[1024,64]{0,1:T(8,128)S(1)} fusion(bf16[7168,64]{0,1:T(8,128)(2,1)S(1)} %copy-done, bf16[1,1024,7168]{2,1,0:T(8,128)(2,1)} %param.6), kind=kOutput, calls=%fused_computation | convolution fusion | flops 939524096 | bytes 15859712 | tf_op jit(solution)/shard_map/dot_general | solution.py:13
  20.7 0.0 copy-start.2
  20.7 10.1 %all-gather = f32[2048,64]{0,1:T(8,128)S(1)} all-gather(f32[1024,64]{0,1:T(8,128)S(1)} %fusion), channel_id=2, replica_groups=mesh['query'=8,'tensor'=2,'dp'=2] {'tensor'}, dimensions={0}, use_global_device_ids=true | all-gather | bytes 786432 | tf_op jit(solution)/shard_map/all_gather | solution.py:15
  30.8 0.4 reshape.7
  31.2 0.6 reduce_sum.9
  31.9 0.0 copy-start.1
  31.9 0.0 reduce-scatter.3.cloned.1.call-done
  31.9 2.2 %multiply_convert_fusion = bf16[1024,32,64]{0,2,1:T(8,128)(2,1)S(1)} fusion(f32[1024,64]{0,1:T(8,128)S(1)} %reduce_sum.9, f32[1024,32]{0,1:T(8,128)} %reduce-scatter.3.cloned.1.call-done), kind=kLoop, calls=%fused_computation.2 | loop fusion | flops 4194304 | bytes 4587520 | tf_op jit(solution)/shard_map/convert_element_type | solution.py:21
  34.1 0.0 copy-done.2
  34.1 2.0 %convolution_convert_fusion = bf16[32,2048]{1,0:T(8,128)(2,1)} fusion(bf16[1024,2048]{0,1:T(8,128)(2,1)S(1)} %bitcast.15, s32[1024]{0:T(1024)S(1)} %bitcast.16), kind=kOutput, calls=%fused_computation.5 | convolution fusion | flops 134316032 | bytes 4329472 | tf_op jit(solution)/shard_map/dot_general | solution.py:24
  36.1 0.0 all-gather.3.cloned.1.call-update
  36.1 0.0 reduce-scatter.5.cloned.1.call-start
  36.2 43.1 %all-gather.3.cloned.1.call-done = bf16[512,2048]{1,0:T(8,128)(2,1)} async-done(((bf16[32,2048]{1,0:T(8,128)(2,1)}), bf16[512,2048]{1,0:T(8,128)(2,1)}) %all-gather.3.cloned.1.call-update) | async-done | bytes 2097168 | tf_op jit(solution)/shard_map/all_gather | solution.py:26
  79.2 0.0 copy-done.1
  79.2 3.0 %fusion.5 = f32[512,64]{0,1:T(8,128)} fusion(bf16[512,2048]{1,0:T(8,128)(2,1)} %all-gather.3.cloned.1.call-done, bf16[64,2048]{1,0:T(8,128)(2,1)S(1)} %copy-done.1), kind=kOutput, calls=%fused_computation.8 | convolution fusion | flops 134217728 | bytes 2490368 | tf_op jit(solution)/shard_map/dot_general | solution.py:25
  82.2 0.0 reduce-scatter.5.cloned.1.call-update
  82.3 9.2 %reduce-scatter.5.cloned.1.call-done = f32[256,64]{0,1:T(8,128)} async-done(((f32[512,64]{0,1:T(8,128)}), f32[256,64]{0,1:T(8,128)}) %reduce-scatter.5.cloned.1.call-update) | async-done | bytes 65552 | tf_op jit(solution)/shard_map/reduce_scatter | solution.py:31
Async XLA Ops:
  6.5 4.5 %copy-start = (bf16[7168,64]{0,1:T(8,128)(2,1)S(1)}, bf16[7168,64]{0,1:T(8,128)(2,1)}, u32[]{:S(2)}) copy-start(bf16[7168,64]{0,1:T(8,128)(2,1)} %param.8) | copy-start | bytes 2752516
  6.5 25.4 %reduce-scatter.3.cloned.1.call-start = ((), (), s32[]{:S(2)}) async-start(), calls=%async_computation.2 | async-start | bytes 393216 | tf_op jit(solution)/shard_map/reduce_scatter | solution.py:17
  10.9 68.3 %all-gather.3.cloned.1.call-start = ((), (), s32[]{:S(2)}) async-start(), calls=%async_computation.3 | async-start | bytes 2228224 | tf_op jit(solution)/shard_map/all_gather | solution.py:26
  20.7 13.4 %copy-start.2 = (s32[1,1024]{1,0:T(1,128)S(1)}, s32[1,1024]{1,0:T(1,128)}, u32[]{:S(2)}) copy-start(s32[1,1024]{1,0:T(1,128)} %param.10) | copy-start | bytes 12292
  31.9 47.4 %copy-start.1 = (bf16[64,2048]{1,0:T(8,128)(2,1)S(1)}, bf16[64,2048]{1,0:T(8,128)(2,1)}, u32[]{:S(2)}) copy-start(bf16[64,2048]{1,0:T(8,128)(2,1)} %param.11) | copy-start | bytes 786436
  36.1 55.4 %reduce-scatter.5.cloned.1.call-start = ((), (), s32[]{:S(2)}) async-start(), calls=%async_computation.4 | async-start | bytes 196608 | tf_op jit(solution)/shard_map/reduce_scatter | solution.py:31
Sparse Core Ops, SparseCore 0:
  11.1 14.4 reduce-scatter.2
  36.2 42.9 all-gather.2
  82.4 9.0 reduce-scatter.4
